TPU v7x, 32 devices: a whole 2x2x4 slice. The times are simulated.
32 devices in a mesh: seq: 8 (over y, x, core), mp: 4 (over z).
Axes of the slice: x: 2, y: 2, z: 4, core: 2. Of those that a mesh axis runs over, the one named last changes fastest.
Arguments:
- stream: float32 [4096, 2048], P('seq', 'mp'), may hold values from -6 to 6
- doc_starts: int32 [4096], P('seq'), may hold values 0 or 1
- gain_first: float32 [2048], replicated, may hold values from 0.5 to 1.5
- proj_inner: bfloat16 [2048, 2560], P(None, 'mp'), may hold values from -0.125 to 0.125
- proj_gate: bfloat16 [2048, 2560], P(None, 'mp'), may hold values from -0.125 to 0.125
- conv_weight: float32 [4, 2560], P(None, 'mp'), may hold values from -3 to 3
- conv_bias: float32 [2560], P('mp'), may hold values from -3 to 3
- gate_recur: bfloat16 [16, 160, 160], P('mp'), may hold values from -0.5 to 0.5
- gate_input: bfloat16 [16, 160, 160], P('mp'), may hold values from -0.5 to 0.5
- bias_recur: float32 [2560], P('mp'), may hold values from -3 to 3
- bias_input: float32 [2560], P('mp'), may hold values from -3 to 3
- decay_param: float32 [2560], P('mp'), may hold values from 3.4 to 15, as said below
- proj_out: bfloat16 [2560, 2048], P('mp'), may hold values from -0.25 to 0.25
- gain_second: float32 [2048], replicated, may hold values from 0.5 to 1.5
- mlp_gate: bfloat16 [2048, 6144], P(None, 'mp'), may hold values from -0.125 to 0.125
- mlp_up: bfloat16 [2048, 6144], P(None, 'mp'), may hold values from -0.125 to 0.125
- mlp_down: bfloat16 [6144, 2048], P('mp'), may hold values from -0.15625 to 0.15625
- cotangent: float32 [4096, 2048], P('seq', 'mp'), may hold values from -6 to 6
Outputs:
- output: float32 [4096, 2048], P('seq', 'mp')
- grad_stream: float32 [4096, 2048], P('seq', 'mp')
- grad_gain_first: float32 [2048], replicated
- grad_proj_inner: float32 [2048, 2560], P('seq', 'mp')
- grad_proj_gate: float32 [2048, 2560], P('seq', 'mp')
- grad_conv_weight: float32 [4, 2560], P(None, 'mp')
- grad_conv_bias: float32 [2560], P('mp')
- grad_gate_recur: float32 [16, 160, 160], P('mp')
- grad_gate_input: float32 [16, 160, 160], P('mp')
- grad_bias_recur: float32 [2560], P('mp')
- grad_bias_input: float32 [2560], P('mp')
- grad_decay: float32 [2560], P('mp')
- grad_proj_out: float32 [2560, 2048], P(('mp', 'seq'))
- grad_gain_second: float32 [2048], replicated
- grad_mlp_gate: float32 [2048, 6144], P('seq', 'mp')
- grad_mlp_up: float32 [2048, 6144], P('seq', 'mp')
- grad_mlp_down: float32 [6144, 2048], P(('mp', 'seq'))
Inputs may be any that keep to these rules, and one draw needn't show every extreme that they name: decay_param is -log(exp(q) - 1) for a per-channel rate q between 0.05 / 4096 and 0.03. `doc_starts`: a 1 marks the first token of a document.
All inputs are finite; a program needn't handle non-finite values. No bound on the sum of `doc_starts` on one device may be relied on, other than what follows from the above.
Results may differ from a plain program's by a relative error of at most 0.0089.
Values sent between devices are 32-bit elements; how exact they have to be, the bound alone decides.
No kernel may reach another device: no remote copies, remote signals or barrier semaphores. Data moves between devices by JAX's collectives and lax.ppermute only.
A program may use at most 256 MiB of HBM per device.

v0:
```python
from functools import partial
import jax
import jax.numpy as jnp
from jax import lax
from jax.sharding import PartitionSpec as P

recur_scale = 8.0
norm_eps = 1e-06


def passed_along(value, axis, steps):
    count = lax.axis_size(axis)
    first, last = (max(0, -steps), min(count, count - steps))
    return lax.ppermute(value, axis, [(source, source + steps) for source in range(first, last)])


def carried_in(value, axis, join, neutral, backward):
    count, mine = (lax.axis_size(axis), lax.axis_index(axis))
    pieces = jax.tree.map(lambda part: lax.all_gather(part, axis), value)
    if backward:
        pieces = jax.tree.map(lambda part: part[::-1], pieces)
        mine = count - 1 - mine
    running = jax.tree.map(
        lambda part, zero: jnp.full_like(part, 0) + jnp.asarray(zero, part.dtype), value, neutral
    )

    def turn(position, running):
        longer = join(running, jax.tree.map(lambda part: part[position], pieces))
        return jax.tree.map(lambda new, old: jnp.where(position < mine, new, old), longer, running)

    return lax.fori_loop(0, count - 1, turn, running)


def norm_rows(rows, gain):
    return rows * lax.rsqrt(jnp.mean(rows * rows, axis=-1, keepdims=True) + norm_eps) * gain


def matmul(left, right):
    return jnp.dot(left, right, preferred_element_type=jnp.float32)


def matmul_nt(left, right):
    return lax.dot_general(
        left, right, (((1,), (1,)), ((), ())), preferred_element_type=jnp.float32
    )


def matmul_tn(left, right):
    return lax.dot_general(
        left, right, (((0,), (0,)), ((), ())), preferred_element_type=jnp.float32
    )


def block_apply(values, weights):
    count = values.shape[0]
    groups = weights.shape[0]
    width = weights.shape[1]
    split = values.reshape(count, groups, width)
    mixed = jnp.einsum("tbi,bio->tbo", split, weights, preferred_element_type=jnp.float32)
    return mixed.reshape(count, groups * width)


def block_back(grads, weights):
    count = grads.shape[0]
    groups = weights.shape[0]
    width = weights.shape[1]
    split = grads.reshape(count, groups, width)
    mixed = jnp.einsum("tbo,bio->tbi", split, weights, preferred_element_type=jnp.float32)
    return mixed.reshape(count, groups * width)


def block_grad(values, grads, groups):
    count = values.shape[0]
    width = values.shape[1] // groups
    left = values.reshape(count, groups, width)
    right = grads.reshape(count, groups, width)
    return jnp.einsum("tbi,tbo->bio", left, right, preferred_element_type=jnp.float32)


def link(earlier, later):
    return (later[0] * earlier[0], later[0] * earlier[1] + later[1])


def local_scan(starts, conv_out, recur_pre, input_pre, decay):
    recur = jax.nn.sigmoid(recur_pre)
    entry = jax.nn.sigmoid(input_pre)
    log_decay = -recur_scale * recur * jax.nn.softplus(-decay)
    factor = starts + (1.0 - starts) * jnp.sqrt(-jnp.expm1(2.0 * log_decay))
    carry = jnp.exp(log_decay) * (1.0 - starts)
    fresh = factor * entry * conv_out
    return lax.associative_scan(link, (carry, fresh), axis=0)


def body(
    stream,
    doc_starts,
    gain_first,
    proj_inner,
    proj_gate,
    conv_weight,
    conv_bias,
    gate_recur,
    gate_input,
    bias_recur,
    bias_input,
    decay_param,
    proj_out,
    gain_second,
    mlp_gate,
    mlp_up,
    mlp_down,
    cotangent,
):
    count = stream.shape[0]
    own_width = stream.shape[1]
    inner_width = proj_inner.shape[1]
    ffn_width = mlp_gate.shape[1]
    groups = gate_recur.shape[0]
    lag = conv_weight.shape[0] - 1
    column = lax.axis_index("mp") * own_width
    rows_full = lax.all_gather(stream, "mp", axis=1, tiled=True)
    first_norm, first_back = jax.vjp(norm_rows, rows_full, gain_first)
    first_low = first_norm.astype(jnp.bfloat16)
    inner = matmul(first_low, proj_inner)
    gate_pre = matmul(first_low, proj_gate)
    starts = doc_starts.astype(jnp.float32)[:, None]
    keep = 1.0 - starts
    tail_keep = jnp.concatenate([keep[count - lag + 1 :], jnp.ones((1, 1), jnp.float32)], 0)
    tail_mask = jnp.flip(jnp.cumprod(jnp.flip(tail_keep, 0), 0), 0)
    prior = passed_along(inner[count - lag :] * tail_mask, "seq", 1)
    ext_inner = jnp.concatenate([prior, inner], 0)
    ext_keep = jnp.concatenate([jnp.ones((lag, 1), jnp.float32), keep], 0)
    valid = jnp.ones((count, 1), jnp.float32)
    valids = []
    conv_out = conv_weight[0] * inner
    for k in range(1, lag + 1):
        valid = valid * ext_keep[lag - k + 1 : lag - k + 1 + count]
        valids.append(valid)
        conv_out = conv_out + conv_weight[k] * ext_inner[lag - k : lag - k + count] * valid
    conv_out = conv_out + conv_bias
    conv_low = conv_out.astype(jnp.bfloat16)
    recur_pre = block_apply(conv_low, gate_recur) + bias_recur
    input_pre = block_apply(conv_low, gate_input) + bias_input
    scan_fn = partial(local_scan, starts)
    (span, partial_state), scan_back = jax.vjp(scan_fn, conv_out, recur_pre, input_pre, decay_param)
    identity = (jnp.ones((inner_width,), jnp.float32), jnp.zeros((inner_width,), jnp.float32))
    entering = carried_in(
        (span[count - 1], partial_state[count - 1]), "seq", link, identity, False
    )[1]
    states = span * entering + partial_state
    gated, gelu_back = jax.vjp(jax.nn.gelu, gate_pre)
    mixed_low = (gated * states).astype(jnp.bfloat16)
    branch = lax.psum(matmul(mixed_low, proj_out), "mp")
    resid = rows_full + branch
    second_norm, second_back = jax.vjp(norm_rows, resid, gain_second)
    second_low = second_norm.astype(jnp.bfloat16)
    ffn_gate = matmul(second_low, mlp_gate)
    ffn_up = matmul(second_low, mlp_up)
    ffn_act, act_back = jax.vjp(jax.nn.gelu, ffn_gate)
    hidden_low = (ffn_act * ffn_up).astype(jnp.bfloat16)
    mlp_own = lax.psum_scatter(matmul(hidden_low, mlp_down), "mp", scatter_dimension=1, tiled=True)
    output = lax.dynamic_slice_in_dim(resid, column, own_width, 1) + mlp_own
    cot_full = lax.all_gather(cotangent, "mp", axis=1, tiled=True)
    cot_low = cot_full.astype(jnp.bfloat16)
    d_hidden = matmul_nt(cot_low, mlp_down)
    d_gate_ffn = act_back(d_hidden * ffn_up)[0]
    d_pair_low = jnp.concatenate([d_gate_ffn, d_hidden * ffn_act], 1).astype(jnp.bfloat16)
    d_second_part = matmul_nt(d_pair_low[:, :ffn_width], mlp_gate) + matmul_nt(
        d_pair_low[:, ffn_width:], mlp_up
    )
    d_second = lax.psum(d_second_part, "mp")
    d_resid_norm, d_gain_second = second_back(d_second)
    d_resid = cot_full + d_resid_norm
    branch_low = d_resid.astype(jnp.bfloat16)
    d_mixed = matmul_nt(branch_low, proj_out)
    d_states = d_mixed * gated
    d_gate_low = gelu_back(d_mixed * states)[0].astype(jnp.bfloat16)
    outgoing = jnp.sum(d_states * span, axis=0)
    incoming = carried_in((span[count - 1], outgoing), "seq", link, identity, True)[1]
    d_total = d_states.at[count - 1].add(incoming)
    d_conv_direct, d_recur, d_input, d_decay = scan_back((d_total * entering, d_total))
    d_recur_low = d_recur.astype(jnp.bfloat16)
    d_input_low = d_input.astype(jnp.bfloat16)
    d_conv = (
        d_conv_direct + block_back(d_recur_low, gate_recur) + block_back(d_input_low, gate_input)
    )
    grad_gate_recur = block_grad(conv_low, d_recur_low, groups)
    grad_gate_input = block_grad(conv_low, d_input_low, groups)
    grad_bias_recur = jnp.sum(d_recur_low.astype(jnp.float32), axis=0)
    grad_bias_input = jnp.sum(d_input_low.astype(jnp.float32), axis=0)
    ext_grad = (
        jnp.zeros((count + lag, inner_width), jnp.float32).at[lag:].add(conv_weight[0] * d_conv)
    )
    conv_terms = [jnp.sum(d_conv * inner, axis=0)]
    for k in range(1, lag + 1):
        weighted = d_conv * valids[k - 1]
        ext_grad = ext_grad.at[lag - k : lag - k + count].add(conv_weight[k] * weighted)
        conv_terms.append(jnp.sum(weighted * ext_inner[lag - k : lag - k + count], axis=0))
    grad_conv_weight = jnp.stack(conv_terms, 0)
    grad_conv_bias = jnp.sum(d_conv, axis=0)
    returned = passed_along(ext_grad[:lag], "seq", -1)
    d_inner = ext_grad[lag:].at[count - lag :].add(returned * tail_mask)
    d_inner_low = d_inner.astype(jnp.bfloat16)
    first_pair_low = jnp.concatenate([d_inner_low, d_gate_low], 1)
    d_first_part = matmul_nt(d_inner_low, proj_inner) + matmul_nt(d_gate_low, proj_gate)
    d_first = lax.psum(d_first_part, "mp")
    d_rows_norm, d_gain_first = first_back(d_first)
    grad_stream = lax.dynamic_slice_in_dim(d_resid + d_rows_norm, column, own_width, 1)
    small = lax.psum(
        (
            d_gain_first,
            d_gain_second,
            grad_conv_weight,
            grad_conv_bias,
            grad_gate_recur,
            grad_gate_input,
            grad_bias_recur,
            grad_bias_input,
            d_decay,
        ),
        "seq",
    )
    grad_first, grad_out, grad_pair, grad_down = (
        lax.psum_scatter(
            matmul_tn(first_low, first_pair_low), "seq", scatter_dimension=0, tiled=True
        ),
        lax.psum_scatter(matmul_tn(mixed_low, branch_low), "seq", scatter_dimension=0, tiled=True),
        lax.psum_scatter(matmul_tn(second_low, d_pair_low), "seq", scatter_dimension=0, tiled=True),
        lax.psum_scatter(matmul_tn(hidden_low, cot_low), "seq", scatter_dimension=0, tiled=True),
    )
    return (
        output,
        grad_stream,
        small[0],
        grad_first[:, :inner_width],
        grad_first[:, inner_width:],
        small[2],
        small[3],
        small[4],
        small[5],
        small[6],
        small[7],
        small[8],
        grad_out,
        small[1],
        grad_pair[:, :ffn_width],
        grad_pair[:, ffn_width:],
        grad_down,
    )


def solution(mesh):
    in_specs = (
        P("seq", "mp"),
        P("seq"),
        P(),
        P(None, "mp"),
        P(None, "mp"),
        P(None, "mp"),
        P("mp"),
        P("mp", None, None),
        P("mp", None, None),
        P("mp"),
        P("mp"),
        P("mp"),
        P("mp", None),
        P(),
        P(None, "mp"),
        P(None, "mp"),
        P("mp", None),
        P("seq", "mp"),
    )
    out_specs = (
        P("seq", "mp"),
        P("seq", "mp"),
        P(),
        P("seq", "mp"),
        P("seq", "mp"),
        P(None, "mp"),
        P("mp"),
        P("mp", None, None),
        P("mp", None, None),
        P("mp"),
        P("mp"),
        P("mp"),
        P(("mp", "seq"), None),
        P(),
        P("seq", "mp"),
        P("seq", "mp"),
        P(("mp", "seq"), None),
    )
    return jax.shard_map(body, mesh=mesh, in_specs=in_specs, out_specs=out_specs, check_vma=False)
```

profile of v0, /device:TPU:0, one launch (start us, length us, event | category | flops | bytes accessed | tf_op | source)
XLA Modules:
  0.0 1586.7 jit_solution(3280703168751612168)
XLA Ops:
  10.0 83.1 %all-gather.7.cloned.1.call-done = f32[512,2048]{1,0:T(8,128)} async-done(((f32[512,512]{1,0:T(8,128)}), f32[512,2048]{1,0:T(8,128)}) %all-gather.7.cloned.1.call-update) | async-done | bytes 4194320 | tf_op jit(solution)/shard_map/all_gather | solution.py:121
  103.9 5.4 fusion.68
  121.4 4.7 exponential_multiply_fusion
  127.2 3.1 slice.594
  130.3 4.5 slice.593
  134.8 4.3 slice.592
  139.8 4.2 slice.635
  144.1 4.3 slice.675
  148.3 4.2 slice.636
  219.0 4.8 pad.543
  226.0 4.8 pad.561
  234.6 4.8 pad.560
  240.2 12.3 all-gather.2
  255.1 4.8 pad.542
  260.7 8.2 all-gather.1
  269.5 5.7 while.34
  275.2 7.2 multiply_convert_fusion.4
  283.2 3.8 fusion.113
  287.9 152.0 %all-reduce.129.cloned.1.call-done = f32[512,2048]{1,0:T(8,128)} async-done(((f32[512,2048]{1,0:T(8,128)}), f32[512,2048]{1,0:T(8,128)}) %all-reduce.129.cloned.1.call-update) | async-done | bytes 4194320 | tf_op jit(solution)/shard_map/psum | solution.py:153
  439.9 4.0 multiply_reduce_fusion.4
  446.0 10.0 fusion.115
  456.0 5.1 fusion.114
  461.1 60.2 %all-gather.9.cloned.1.call-done = f32[512,2048]{1,0:T(8,128)} async-done(((f32[512,512]{1,0:T(8,128)}), f32[512,2048]{1,0:T(8,128)}) %all-gather.9.cloned.1.call-update) | async-done | bytes 4194320 | tf_op jit(solution)/shard_map/all_gather | solution.py:163
  521.3 12.5 multiply_convert_fusion.2
  533.8 6.7 fusion.117
  540.6 7.9 convolution_add_fusion.1
  551.2 9.5 fusion.116
  560.8 141.4 %all-reduce.131.cloned.1.call-done = f32[512,2048]{1,0:T(8,128)} async-done(((f32[512,2048]{1,0:T(8,128)}), f32[512,2048]{1,0:T(8,128)}) %all-reduce.131.cloned.1.call-update) | async-done | bytes 4194320 | tf_op jit(solution)/shard_map/psum | solution.py:171
  702.2 5.2 multiply_reduce_fusion
  708.1 4.1 fusion
  712.3 7.2 multiply_reduce_fusion.11
  719.5 9.0 all-gather.3
  732.1 5.7 while.35
  744.1 4.2 slice.680
  748.3 3.5 fusion.72
  751.9 4.2 slice.696
  756.1 3.7 fusion.73
  759.8 4.3 slice.681
  764.1 4.2 slice.697
  872.6 3.8 multiply_add_fusion.4
  876.4 4.9 pad.680
  886.7 5.1 pad.621
  891.7 4.9 pad.681
  899.8 5.8 multiply_reduce_fusion.6
  922.2 6.3 multiply_reduce_fusion.9
  931.5 4.4 scatter-add.24
  938.9 4.4 scatter-add.25
  943.3 3.1 constant_dynamic-update-slice_fusion
  947.7 3.9 fusion.118
  952.4 6.8 convolution_add_fusion
  959.3 8.6 fusion.25
  968.0 14.3 fusion.8
  988.0 6.0 fusion.30
  994.1 10.6 fusion.34
  1007.6 106.2 %all-reduce.133.cloned.1.call-done = f32[512,2048]{1,0:T(8,128)} async-done(((f32[512,2048]{1,0:T(8,128)}), f32[512,2048]{1,0:T(8,128)}) %all-reduce.133.cloned.1.call-update) | async-done | bytes 4194320 | tf_op jit(solution)/shard_map/psum | solution.py:206
  1113.8 6.4 multiply_reduce_fusion.1
  1120.2 25.1 %all-reduce.122 = (f32[2048]{0:T(1024)}, f32[4,640]{1,0:T(4,128)}, f32[640]{0:T(1024)}, f32[640]{0:T(1024)}, f32[640]{0:T(1024)}, /*index=5*/f32[640]{0:T(1024)}, f32[2048]{0:T(1024)}) all-reduce(f32[2048]{0:T(1024)S(1)} %get-tuple-element.317, f32[4,640]{1,0:T(4,128)S(1)} %pad_maximum_fusion.15, ...), channel_id=1, replica_groups=mesh['seq'=8,'mp'=4] {'seq'}, use_global_device_ids=true, to_apply=%region_15.16 | all-reduce | flops 9216 | bytes 73728 | tf_op jit(solution)/shard_map/psum | solution.py:209
  1145.3 3.1 fusion.29
  1148.4 49.5 %reduce-scatter.8.cloned.1.call-done = f32[256,1280]{1,0:T(8,128)} async-done(((f32[2048,1280]{1,0:T(8,128)}), f32[256,1280]{1,0:T(8,128)}) %reduce-scatter.8.cloned.1.call-update) | async-done | bytes 1310736 | tf_op jit(solution)/shard_map/reduce_scatter | solution.py:224
  1200.3 158.1 %reduce-scatter.12.cloned.1.call-done = f32[256,3072]{1,0:T(8,128)} async-done(((f32[2048,3072]{1,0:T(8,128)}), f32[256,3072]{1,0:T(8,128)}) %reduce-scatter.12.cloned.1.call-update) | async-done | bytes 3145744 | tf_op jit(solution)/shard_map/reduce_scatter | solution.py:228
  1358.4 3.7 fusion.69
  1362.1 58.5 %all-reduce.135.cloned.1.call-done = (f32[4,160,160]{2,1,0:T(8,128)}, f32[4,160,160]{2,1,0:T(8,128)}) async-done(((f32[4,160,160]{2,1,0:T(8,128)}, f32[4,160,160]{2,1,0:T(8,128)}), (f32[4,160,160]{2,1,0:T(8,128)}, f32[4,160,160]{2,1,0:T(8,128)})) %all-reduce.135.cloned.1.call-update) | async-done | bytes 819216 | tf_op jit(solution)/shard_map/psum | solution.py:209
  1420.6 60.0 %reduce-scatter.10.cloned.1.call-done = f32[80,2048]{1,0:T(8,128)} async-done(((f32[640,2048]{1,0:T(8,128)}), f32[80,2048]{1,0:T(8,128)}) %reduce-scatter.10.cloned.1.call-update) | async-done | bytes 655376 | tf_op jit(solution)/shard_map/reduce_scatter | solution.py:227
  1480.6 96.5 %reduce-scatter.14.cloned.1.call-done = f32[192,2048]{1,0:T(8,128)} async-done(((f32[1536,2048]{1,0:T(8,128)}), f32[192,2048]{1,0:T(8,128)}) %reduce-scatter.14.cloned.1.call-update) | async-done | bytes 1572880 | tf_op jit(solution)/shard_map/reduce_scatter | solution.py:229
  (778 shorter events, 281.8 us)
Async XLA Ops:
  7.2 268.0 %copy-start = (bf16[2048,640]{1,0:T(8,128)(2,1)S(1)}, bf16[2048,640]{1,0:T(8,128)(2,1)}, u32[]{:S(2)}) copy-start(bf16[2048,640]{1,0:T(8,128)(2,1)} %param.38) | copy-start | bytes 7864324
  7.2 85.9 %all-gather.7.cloned.1.call-start = ((), (), s32[]{:S(2)}) async-start(), calls=%async_computation.5 | async-start | bytes 5242880 | tf_op jit(solution)/shard_map/all_gather | solution.py:121
  7.9 431.9 %all-reduce.129.cloned.1.call-start = ((), (), s32[]{:S(2)}) async-start(), calls=%async_computation.6 | async-start | bytes 8388608 | tf_op jit(solution)/shard_map/psum | solution.py:153
  8.7 112.7 %copy-start.115 = (f32[512]{0:T(512)}, f32[512]{0:T(512)S(1)}, u32[]{:S(2)}) copy-start(f32[512]{0:T(512)S(1)} %broadcast_subtract_fusion) | copy-start | bytes 6148
  9.2 90.9 %copy-start.180 = (f32[3,1]{0,1:T(1,128)}, f32[3,1]{0,1:T(1,128)S(1)}, u32[]{:S(2)}) copy-start(f32[3,1]{0,1:T(1,128)S(1)} %rev.14) | copy-start | bytes 40
  9.3 94.6 %copy-start.160 = (f32[512,1]{0,1:T(1,128)}, f32[512,1]{0,1:T(1,128)S(1)}, u32[]{:S(2)}) copy-start(f32[512,1]{0,1:T(1,128)S(1)} %get-tuple-element.399) | copy-start | bytes 6148
  9.3 94.6 %copy-start.162 = (f32[512,1]{0,1:T(1,128)}, f32[512,1]{0,1:T(1,128)S(1)}, u32[]{:S(2)}) copy-start(f32[512,1]{0,1:T(1,128)S(1)} %get-tuple-element.400) | copy-start | bytes 6148
  9.3 86.5 %copy-start.164 = (f32[2048]{0:T(1024)S(1)}, f32[2048]{0:T(1024)}, u32[]{:S(2)}) copy-start(f32[2048]{0:T(1024)} %param.36) | copy-start | bytes 24580
  10.0 111.4 %copy-start.117 = (f32[640]{0:T(1024)}, f32[640]{0:T(1024)S(1)}, u32[]{:S(2)}) copy-start(f32[640]{0:T(1024)S(1)} %broadcast_multiply_fusion.3) | copy-start | bytes 7684
  101.3 2.6 collective-permute-start
  103.6 17.7 %copy-start.166 = (f32[512]{0:T(512)}, f32[512]{0:T(512)S(1)}, u32[]{:S(2)}) copy-start(f32[512]{0:T(512)S(1)} %convert_element_type.44) | copy-start | bytes 6148
  130.3 22.3 %copy-start.17 = (f32[256,640]{1,0:T(8,128)}, f32[256,640]{1,0:T(8,128)S(1)}, u32[]{:S(2)}) copy-start(f32[256,640]{1,0:T(8,128)S(1)} %slice.594) | copy-start | bytes 1966084
  155.0 9.3 copy-start.28
  176.7 8.4 copy-start.61
  185.1 8.0 copy-start.39
  186.5 8.4 copy-start.41
  189.9 9.7 copy-start.22
  275.2 8.1 copy-start.182
  287.1 234.3 %all-gather.9.cloned.1.call-start = ((), (), s32[]{:S(2)}) async-start(), calls=%async_computation.8 | async-start | bytes 5242880 | tf_op jit(solution)/shard_map/all_gather | solution.py:163
  287.8 156.1 %copy-start.129 = (f32[2048]{0:T(1024)S(1)}, f32[2048]{0:T(1024)}, u32[]{:S(2)}) copy-start(f32[2048]{0:T(1024)} %param.47) | copy-start | bytes 24580
  287.8 414.3 %all-reduce.131.cloned.1.call-start = ((), (), s32[]{:S(2)}) async-start(), calls=%async_computation.9 | async-start | bytes 8388608 | tf_op jit(solution)/shard_map/psum | solution.py:171
  443.9 12.1 slice-start.14
  446.0 10.0 copy-start.46
  446.0 10.0 slice-start.15
  548.5 456.3 %reduce-scatter.6.cloned.1.call-start = ((), (), s32[]{:S(2)}) async-start(), calls=%async_computation.7 | async-start | bytes 5242880 | tf_op jit(solution)/shard_map/reduce_scatter | solution.py:161
  560.7 141.5 %copy-start.170 = (f32[512]{0:T(512)S(1)}, f32[512]{0:T(512)}, u32[]{:S(2)}) copy-start(f32[512]{0:T(512)} %copy-done.169) | copy-start | bytes 6148
  560.7 553.0 %all-reduce.133.cloned.1.call-start = ((), (), s32[]{:S(2)}) async-start(), calls=%async_computation.10 | async-start | bytes 8388608 | tf_op jit(solution)/shard_map/psum | solution.py:206
  759.8 8.6 copy-start.38
  799.5 8.9 copy-start.95
  799.5 8.9 copy-start.97
  801.1 8.8 copy-start.109
  803.3 14.4 copy-start.36
  804.9 11.1 copy-start.114
  807.5 10.2 copy-start.119
  808.4 9.4 copy-start.120
  809.8 8.0 copy-start.135
  817.8 7.5 copy-start.93
  825.3 7.8 copy-start.66
  825.3 7.8 copy-start.68
  825.3 7.8 slice-start.8
  825.3 7.8 slice-start.9
  827.1 11.4 copy-start.64
  829.7 12.3 copy-start.92
  831.0 12.4 copy-start.49
  831.0 12.4 copy-start.51
  831.0 12.4 slice-start.6
  831.0 12.4 slice-start.7
  845.5 9.5 copy-start.70
  847.0 9.5 copy-start.33
  847.0 9.5 slice-start.4
  847.0 9.5 slice-start.5
  865.4 7.2 slice-start.2
  865.4 7.2 slice-start.3
  946.4 5.3 collective-permute-start.1
  959.3 238.6 %reduce-scatter.8.cloned.1.call-start = ((), (), s32[]{:S(2)}) async-start(), calls=%async_computation.11 | async-start | bytes 11796480 | tf_op jit(solution)/shard_map/reduce_scatter | solution.py:224
  967.9 390.5 %reduce-scatter.12.cloned.1.call-start = ((), (), s32[]{:S(2)}) async-start(), calls=%async_computation.13 | async-start | bytes 28311552 | tf_op jit(solution)/shard_map/reduce_scatter | solution.py:228
  982.3 438.3 %all-reduce.135.cloned.1.call-start = ((), (), s32[]{:S(2)}) async-start(), calls=%async_computation.15 | async-start | bytes 2621440 | tf_op jit(solution)/shard_map/psum | solution.py:209
  986.9 493.7 %reduce-scatter.10.cloned.1.call-start = ((), (), s32[]{:S(2)}) async-start(), calls=%async_computation.12 | async-start | bytes 5898240 | tf_op jit(solution)/shard_map/reduce_scatter | solution.py:227
  994.1 583.0 %reduce-scatter.14.cloned.1.call-start = ((), (), s32[]{:S(2)}) async-start(), calls=%async_computation.14 | async-start | bytes 14155776 | tf_op jit(solution)/shard_map/reduce_scatter | solution.py:229
  1004.8 108.9 %copy-start.159 = (f32[512]{0:T(512)S(1)}, f32[512]{0:T(512)}, u32[]{:S(2)}) copy-start(f32[512]{0:T(512)} %copy-done.158) | copy-start | bytes 6148
  1004.8 108.9 %copy-start.165 = (f32[2048]{0:T(1024)S(1)}, f32[2048]{0:T(1024)}, u32[]{:S(2)}) copy-start(f32[2048]{0:T(1024)} %param.36) | copy-start | bytes 24580
  1007.6 112.6 %copy-start.168 = (f32[2048]{0:T(1024)S(1)}, f32[2048]{0:T(1024)}, u32[]{:S(2)}) copy-start(f32[2048]{0:T(1024)} %get-tuple-element.315) | copy-start | bytes 24580
  1007.6 137.7 %copy-start.173 = (f32[512]{0:T(512)S(1)}, f32[512]{0:T(512)}, u32[]{:S(2)}) copy-start(f32[512]{0:T(512)} %copy-done.172) | copy-start | bytes 6148
  1420.6 158.5 %copy-start.72 = (f32[4,160,160]{2,1,0:T(8,128)S(1)}, f32[4,160,160]{2,1,0:T(8,128)}, u32[]{:S(2)}) copy-start(f32[4,160,160]{2,1,0:T(8,128)} %get-tuple-element.666) | copy-start | bytes 1228804
  (151 other events, 537.6 us)
Sparse Core Ops, SparseCore 0:
  9.6 83.4 all-gather.6
  287.2 152.6 all-reduce.128
  441.5 79.7 all-gather.8
  548.6 153.4 all-reduce.130
  704.3 75.7 reduce-scatter.5
  959.4 154.2 all-reduce.132
  1117.2 80.5 reduce-scatter.7
  1201.5 156.8 reduce-scatter.11
  1362.8 57.8 all-reduce.134
  1424.8 55.7 reduce-scatter.9
  1484.7 92.3 reduce-scatter.13
where the time goes:
time: 1600 us; the launch traced here: 1590 us
  waiting for transfers between devices  967 us (60%)
  local copies, waits for them, and re-layouts  262 us (16%)
  other arithmetic  146 us (9%)
  matrix products  136 us (8%)
  blocking collectives  54.6 us (3%)
  between operations  16.9 us (1%)
    reduce_scatter x1, waiting for transfers between devices, body(): lax.psum_scatter(matmul_tn(second_low, d_pair_low), 'seq', scatter_dimens...  158 us
    psum x1, waiting for transfers between devices, body(): branch = lax.psum(matmul(mixed_low, proj_out), 'mp')  152 us
    psum x1, waiting for transfers between devices, body(): d_second = lax.psum(d_second_part, 'mp')  141 us
    pad x94, local copies, waits for them, and re-layouts, local_scan(): return lax.associative_scan(link, (carry, fresh), axis=0)  112 us
    psum x1, waiting for transfers between devices, body(): d_first = lax.psum(d_first_part, 'mp')  106 us
    reduce_scatter x1, waiting for transfers between devices, body(): lax.psum_scatter(matmul_tn(hidden_low, cot_low), 'seq', scatter_dimension...  96.5 us
    all_gather x1, waiting for transfers between devices, body(): rows_full = lax.all_gather(stream, 'mp', axis=1, tiled=True)  83.1 us
    slice x92, local copies, waits for them, and re-layouts, local_scan(): return lax.associative_scan(link, (carry, fresh), axis=0)  81.5 us
  transfers between devices with their start and end apart: 13, of which 11 were waited for; matrix products, arithmetic and copies ran while one was open for 21% of the time, Pallas kernels for 0%

commit v1 on v0

--- a/solution.py
+++ b/solution.py
@@ -6,6 +6,19 @@
 
 recur_scale = 8.0
 norm_eps = 1e-06
+
+
+def _update_keys(panel):
+    chips = lax.axis_size("mp")
+    found_now = sorted(((no, (no + 1) % chips) for no in range(chips)))
+    r1 = panel
+    shelf = [r1]
+    for t in [*range(1, chips)]:
+        r1 = lax.ppermute(r1, perm=found_now, axis_name="mp")
+        shelf.insert(0, r1)
+    heard = jnp.concatenate(shelf, 1)
+    odd = lax.axis_index("mp") + 1
+    return jnp.roll(heard, odd * panel.shape[1], axis=1)
 
 
 def passed_along(value, axis, steps):
@@ -118,7 +131,7 @@
     groups = gate_recur.shape[0]
     lag = conv_weight.shape[0] - 1
     column = lax.axis_index("mp") * own_width
-    rows_full = lax.all_gather(stream, "mp", axis=1, tiled=True)
+    rows_full = _update_keys(stream)
     first_norm, first_back = jax.vjp(norm_rows, rows_full, gain_first)
     first_low = first_norm.astype(jnp.bfloat16)
     inner = matmul(first_low, proj_inner)

time: 1600 us -> 1600 us (level)
    all_gather x1 -> x0, waiting for transfers between devices: 83.1 us -> none  [body(): rows_full = lax.all_gather(stream, 'mp', axis=1, tiled=True)]
    ppermute x0 -> x3, waiting for transfers between devices: none -> 75.2 us  [_update_keys(): r1 = lax.ppermute(r1, perm=found_now, axis_name='mp')]
  transfers between devices with their start and end apart: 13 -> 15, of which waited for: 11 -> 13; matrix products, arithmetic and copies ran while one was open for 21% -> 21% of each run, Pallas kernels for 0% -> 0%
where the time goes in v1:
time: 1600 us; the launch traced here: 1590 us
  waiting for transfers between devices  958 us (60%)
  local copies, waits for them, and re-layouts  272 us (17%)
  other arithmetic  143 us (9%)
  matrix products  136 us (8%)
  blocking collectives  54.6 us (3%)
  between operations  17.2 us (1%)
    reduce_scatter x1, waiting for transfers between devices, body(): lax.psum_scatter(matmul_tn(second_low, d_pair_low), 'seq', scatter_dimens...  158 us
    psum x1, waiting for transfers between devices, body(): branch = lax.psum(matmul(mixed_low, proj_out), 'mp')  152 us
    psum x1, waiting for transfers between devices, body(): d_second = lax.psum(d_second_part, 'mp')  141 us
    pad x94, local copies, waits for them, and re-layouts, local_scan(): return lax.associative_scan(link, (carry, fresh), axis=0)  112 us
    psum x1, waiting for transfers between devices, body(): d_first = lax.psum(d_first_part, 'mp')  106 us
    reduce_scatter x1, waiting for transfers between devices, body(): lax.psum_scatter(matmul_tn(hidden_low, cot_low), 'seq', scatter_dimension...  96.4 us
    slice x92, local copies, waits for them, and re-layouts, local_scan(): return lax.associative_scan(link, (carry, fresh), axis=0)  81.5 us
    ppermute x3, waiting for transfers between devices, _update_keys(): r1 = lax.ppermute(r1, perm=found_now, axis_name='mp')  75.2 us
  transfers between devices with their start and end apart: 15, of which 13 were waited for; matrix products, arithmetic and copies ran while one was open for 21% of the time, Pallas kernels for 0%

profile of v1, /device:TPU:0, one launch (start us, length us, event | category | flops | bytes accessed | tf_op | source)
XLA Modules:
  0.0 1586.9 jit_solution(229777817571805726)
XLA Ops:
  10.3 25.4 %collective-permute-done = f32[512,512]{1,0:T(8,128)S(1)} collective-permute-done((f32[512,512]{1,0:T(8,128)}, f32[512,512]{1,0:T(8,128)S(1)}, u32[]{:S(2)}, u32[]{:S(2)}) %collective-permute-start) | collective-permute-done | bytes 1048608 | tf_op jit(solution)/shard_map/ppermute | solution.py:17
  36.7 26.2 %collective-permute-done.1 = f32[512,512]{1,0:T(8,128)} collective-permute-done((f32[512,512]{1,0:T(8,128)S(1)}, f32[512,512]{1,0:T(8,128)}, u32[]{:S(2)}, u32[]{:S(2)}) %collective-permute-start.1) | collective-permute-done | bytes 1048608 | tf_op jit(solution)/shard_map/ppermute | solution.py:17
  65.0 23.5 %collective-permute-done.2 = f32[512,512]{1,0:T(8,128)} collective-permute-done((f32[512,512]{1,0:T(8,128)}, f32[512,512]{1,0:T(8,128)}, u32[]{:S(2)}, u32[]{:S(2)}) %collective-permute-start.2) | collective-permute-done | bytes 1048608 | tf_op jit(solution)/shard_map/ppermute | solution.py:17
  105.0 5.0 fusion.68
  122.2 4.7 exponential_multiply_fusion
  128.0 3.1 slice.594
  131.1 4.5 slice.593
  135.6 4.3 slice.592
  140.6 4.2 slice.635
  144.9 4.3 slice.675
  149.1 4.2 slice.636
  219.8 4.8 pad.543
  226.9 4.8 pad.561
  235.5 4.8 pad.560
  241.1 12.3 all-gather.2
  256.0 4.9 pad.542
  261.6 8.2 all-gather.1
  270.5 5.7 while.34
  276.2 7.2 multiply_convert_fusion.4
  284.2 3.8 fusion.113
  288.8 151.6 %all-reduce.129.cloned.1.call-done = f32[512,2048]{1,0:T(8,128)} async-done(((f32[512,2048]{1,0:T(8,128)}), f32[512,2048]{1,0:T(8,128)}) %all-reduce.129.cloned.1.call-update) | async-done | bytes 4194320 | tf_op jit(solution)/shard_map/psum | solution.py:166
  440.4 4.0 multiply_reduce_fusion.4
  446.5 10.0 fusion.115
  456.5 5.1 fusion.114
  461.6 60.2 %all-gather.6.cloned.1.call-done = f32[512,2048]{1,0:T(8,128)} async-done(((f32[512,512]{1,0:T(8,128)}), f32[512,2048]{1,0:T(8,128)}) %all-gather.6.cloned.1.call-update) | async-done | bytes 4194320 | tf_op jit(solution)/shard_map/all_gather | solution.py:176
  521.8 12.5 multiply_convert_fusion.2
  534.4 6.7 fusion.117
  541.1 8.0 convolution_add_fusion.1
  551.8 9.6 fusion.116
  561.5 141.2 %all-reduce.131.cloned.1.call-done = f32[512,2048]{1,0:T(8,128)} async-done(((f32[512,2048]{1,0:T(8,128)}), f32[512,2048]{1,0:T(8,128)}) %all-reduce.131.cloned.1.call-update) | async-done | bytes 4194320 | tf_op jit(solution)/shard_map/psum | solution.py:184
  702.8 5.2 multiply_reduce_fusion
  708.7 4.1 fusion
  712.9 7.2 multiply_reduce_fusion.11
  720.1 9.0 all-gather.3
  732.7 5.7 while.35
  744.7 4.3 slice.680
  748.9 3.5 fusion.72
  752.4 4.2 slice.696
  756.7 3.7 fusion.73
  760.3 4.3 slice.681
  764.6 4.2 slice.697
  873.2 3.8 multiply_add_fusion.4
  877.0 4.9 pad.680
  887.2 4.9 pad.621
  892.0 4.9 pad.681
  900.1 5.8 multiply_reduce_fusion.6
  922.4 6.1 multiply_reduce_fusion.9
  931.3 4.4 scatter-add.24
  938.8 4.4 scatter-add.25
  947.6 3.9 fusion.118
  952.4 6.9 convolution_add_fusion
  959.3 8.6 fusion.25
  967.9 14.3 fusion.8
  988.0 6.1 fusion.30
  994.2 10.6 fusion.34
  1007.6 106.1 %all-reduce.133.cloned.1.call-done = f32[512,2048]{1,0:T(8,128)} async-done(((f32[512,2048]{1,0:T(8,128)}), f32[512,2048]{1,0:T(8,128)}) %all-reduce.133.cloned.1.call-update) | async-done | bytes 4194320 | tf_op jit(solution)/shard_map/psum | solution.py:219
  1113.8 6.6 multiply_reduce_fusion.1
  1120.4 25.1 %all-reduce.122 = (f32[2048]{0:T(1024)}, f32[4,640]{1,0:T(4,128)}, f32[640]{0:T(1024)}, f32[640]{0:T(1024)}, f32[640]{0:T(1024)}, /*index=5*/f32[640]{0:T(1024)}, f32[2048]{0:T(1024)}) all-reduce(f32[2048]{0:T(1024)S(1)} %get-tuple-element.317, f32[4,640]{1,0:T(4,128)S(1)} %pad_maximum_fusion.15, ...), channel_id=1, replica_groups=mesh['seq'=8,'mp'=4] {'seq'}, use_global_device_ids=true, to_apply=%region_15.16 | all-reduce | flops 9216 | bytes 73728 | tf_op jit(solution)/shard_map/psum | solution.py:222
  1148.6 49.1 %reduce-scatter.8.cloned.1.call-done = f32[256,1280]{1,0:T(8,128)} async-done(((f32[2048,1280]{1,0:T(8,128)}), f32[256,1280]{1,0:T(8,128)}) %reduce-scatter.8.cloned.1.call-update) | async-done | bytes 1310736 | tf_op jit(solution)/shard_map/reduce_scatter | solution.py:237
  1200.2 158.1 %reduce-scatter.12.cloned.1.call-done = f32[256,3072]{1,0:T(8,128)} async-done(((f32[2048,3072]{1,0:T(8,128)}), f32[256,3072]{1,0:T(8,128)}) %reduce-scatter.12.cloned.1.call-update) | async-done | bytes 3145744 | tf_op jit(solution)/shard_map/reduce_scatter | solution.py:241
  1358.3 3.7 fusion.69
  1362.0 58.6 %all-reduce.135.cloned.1.call-done = (f32[4,160,160]{2,1,0:T(8,128)}, f32[4,160,160]{2,1,0:T(8,128)}) async-done(((f32[4,160,160]{2,1,0:T(8,128)}, f32[4,160,160]{2,1,0:T(8,128)}), (f32[4,160,160]{2,1,0:T(8,128)}, f32[4,160,160]{2,1,0:T(8,128)})) %all-reduce.135.cloned.1.call-update) | async-done | bytes 819216 | tf_op jit(solution)/shard_map/psum | solution.py:222
  1420.6 60.1 %reduce-scatter.10.cloned.1.call-done = f32[80,2048]{1,0:T(8,128)} async-done(((f32[640,2048]{1,0:T(8,128)}), f32[80,2048]{1,0:T(8,128)}) %reduce-scatter.10.cloned.1.call-update) | async-done | bytes 655376 | tf_op jit(solution)/shard_map/reduce_scatter | solution.py:240
  1480.7 96.4 %reduce-scatter.14.cloned.1.call-done = f32[192,2048]{1,0:T(8,128)} async-done(((f32[1536,2048]{1,0:T(8,128)}), f32[192,2048]{1,0:T(8,128)}) %reduce-scatter.14.cloned.1.call-update) | async-done | bytes 1572880 | tf_op jit(solution)/shard_map/reduce_scatter | solution.py:242
  (795 shorter events, 296.9 us)
Async XLA Ops:
  7.2 269.0 %copy-start = (bf16[2048,640]{1,0:T(8,128)(2,1)S(1)}, bf16[2048,640]{1,0:T(8,128)(2,1)}, u32[]{:S(2)}) copy-start(bf16[2048,640]{1,0:T(8,128)(2,1)} %param.38) | copy-start | bytes 7864324
  7.2 433.2 %all-reduce.129.cloned.1.call-start = ((), (), s32[]{:S(2)}) async-start(), calls=%async_computation.5 | async-start | bytes 8388608 | tf_op jit(solution)/shard_map/psum | solution.py:166
  7.2 28.5 %collective-permute-start = (f32[512,512]{1,0:T(8,128)}, f32[512,512]{1,0:T(8,128)S(1)}, u32[]{:S(2)}, u32[]{:S(2)}) collective-permute-start(f32[512,512]{1,0:T(8,128)} %param.34), channel_id=1, source_target_pairs={{0,1},{1,2},{2,3},{3,0},{4,5},{5,6},{6,7},{7,4},{8,9},{9,10},{10,1... | collective-permute-start | bytes 3145736 | tf_op jit(solution)/shard_map/ppermute | solution.py:17
  36.7 26.2 %collective-permute-start.1 = (f32[512,512]{1,0:T(8,128)S(1)}, f32[512,512]{1,0:T(8,128)}, u32[]{:S(2)}, u32[]{:S(2)}) collective-permute-start(f32[512,512]{1,0:T(8,128)S(1)} %collective-permute-done), channel_id=1, source_target_pairs={{0,1},{1,2},{2,3},{3,0},{4,5},{5,6},{6,7},{7,4},{8,9},{9,10},{10,1... | collective-permute-start | bytes 3145736 | tf_op jit(solution)/shard_map/ppermute | solution.py:17
  62.9 25.5 %collective-permute-start.2 = (f32[512,512]{1,0:T(8,128)}, f32[512,512]{1,0:T(8,128)}, u32[]{:S(2)}, u32[]{:S(2)}) collective-permute-start(f32[512,512]{1,0:T(8,128)} %collective-permute-done.1), channel_id=1, source_target_pairs={{0,1},{1,2},{2,3},{3,0},{4,5},{5,6},{6,7},{7,4},{8,9},{9,10},{10,1... | collective-permute-start | bytes 3145736 | tf_op jit(solution)/shard_map/ppermute | solution.py:17
  63.6 58.5 %copy-start.118 = (f32[512]{0:T(512)}, f32[512]{0:T(512)S(1)}, u32[]{:S(2)}) copy-start(f32[512]{0:T(512)S(1)} %broadcast_subtract_fusion) | copy-start | bytes 6148
  64.2 37.6 %copy-start.183 = (f32[3,1]{0,1:T(1,128)}, f32[3,1]{0,1:T(1,128)S(1)}, u32[]{:S(2)}) copy-start(f32[3,1]{0,1:T(1,128)S(1)} %rev.14) | copy-start | bytes 40
  64.2 40.8 %copy-start.163 = (f32[512,1]{0,1:T(1,128)}, f32[512,1]{0,1:T(1,128)S(1)}, u32[]{:S(2)}) copy-start(f32[512,1]{0,1:T(1,128)S(1)} %get-tuple-element.399) | copy-start | bytes 6148
  64.2 40.8 %copy-start.165 = (f32[512,1]{0,1:T(1,128)}, f32[512,1]{0,1:T(1,128)S(1)}, u32[]{:S(2)}) copy-start(f32[512,1]{0,1:T(1,128)S(1)} %get-tuple-element.400) | copy-start | bytes 6148
  64.9 57.2 %copy-start.120 = (f32[640]{0:T(1024)}, f32[640]{0:T(1024)S(1)}, u32[]{:S(2)}) copy-start(f32[640]{0:T(1024)S(1)} %broadcast_multiply_fusion.3) | copy-start | bytes 7684
  102.9 2.1 collective-permute-start.3
  104.8 17.4 %copy-start.169 = (f32[512]{0:T(512)}, f32[512]{0:T(512)S(1)}, u32[]{:S(2)}) copy-start(f32[512]{0:T(512)S(1)} %convert_element_type.44) | copy-start | bytes 6148
  131.1 22.3 %copy-start.17 = (f32[256,640]{1,0:T(8,128)}, f32[256,640]{1,0:T(8,128)S(1)}, u32[]{:S(2)}) copy-start(f32[256,640]{1,0:T(8,128)S(1)} %slice.594) | copy-start | bytes 1966084
  155.8 9.3 copy-start.31
  177.5 8.4 copy-start.64
  185.9 8.0 copy-start.42
  187.3 8.3 copy-start.44
  190.7 9.8 copy-start.22
  276.1 8.0 copy-start.185
  288.0 233.9 %all-gather.6.cloned.1.call-start = ((), (), s32[]{:S(2)}) async-start(), calls=%async_computation.7 | async-start | bytes 5242880 | tf_op jit(solution)/shard_map/all_gather | solution.py:176
  288.7 155.7 %copy-start.132 = (f32[2048]{0:T(1024)S(1)}, f32[2048]{0:T(1024)}, u32[]{:S(2)}) copy-start(f32[2048]{0:T(1024)} %param.47) | copy-start | bytes 24580
  288.7 414.0 %all-reduce.131.cloned.1.call-start = ((), (), s32[]{:S(2)}) async-start(), calls=%async_computation.8 | async-start | bytes 8388608 | tf_op jit(solution)/shard_map/psum | solution.py:184
  444.4 12.1 slice-start.14
  446.5 10.0 copy-start.49
  446.5 10.0 slice-start.15
  549.1 455.8 %reduce-scatter.6.cloned.1.call-start = ((), (), s32[]{:S(2)}) async-start(), calls=%async_computation.6 | async-start | bytes 5242880 | tf_op jit(solution)/shard_map/reduce_scatter | solution.py:174
  561.5 141.3 %copy-start.173 = (f32[512]{0:T(512)S(1)}, f32[512]{0:T(512)}, u32[]{:S(2)}) copy-start(f32[512]{0:T(512)} %copy-done.172) | copy-start | bytes 6148
  561.5 552.3 %all-reduce.133.cloned.1.call-start = ((), (), s32[]{:S(2)}) async-start(), calls=%async_computation.9 | async-start | bytes 8388608 | tf_op jit(solution)/shard_map/psum | solution.py:219
  760.3 8.6 copy-start.41
  800.1 8.9 copy-start.98
  800.1 8.9 copy-start.100
  801.7 8.8 copy-start.112
  803.9 14.5 copy-start.39
  805.5 11.1 copy-start.117
  808.1 10.3 copy-start.122
  808.9 9.4 copy-start.123
  810.4 8.0 copy-start.138
  818.4 7.5 copy-start.96
  825.9 7.8 copy-start.69
  825.9 7.8 copy-start.71
  825.9 7.8 slice-start.8
  825.9 7.8 slice-start.9
  827.7 11.3 copy-start.67
  830.4 12.3 copy-start.95
  831.6 12.4 copy-start.52
  831.6 12.4 copy-start.54
  831.6 12.4 slice-start.6
  831.6 12.4 slice-start.7
  846.1 9.5 copy-start.73
  847.6 9.5 copy-start.36
  847.6 9.5 slice-start.4
  847.6 9.5 slice-start.5
  866.0 7.2 slice-start.3
  946.3 5.4 collective-permute-start.4
  959.3 238.5 %reduce-scatter.8.cloned.1.call-start = ((), (), s32[]{:S(2)}) async-start(), calls=%async_computation.10 | async-start | bytes 11796480 | tf_op jit(solution)/shard_map/reduce_scatter | solution.py:237
  967.9 390.4 %reduce-scatter.12.cloned.1.call-start = ((), (), s32[]{:S(2)}) async-start(), calls=%async_computation.12 | async-start | bytes 28311552 | tf_op jit(solution)/shard_map/reduce_scatter | solution.py:241
  982.3 438.3 %all-reduce.135.cloned.1.call-start = ((), (), s32[]{:S(2)}) async-start(), calls=%async_computation.14 | async-start | bytes 2621440 | tf_op jit(solution)/shard_map/psum | solution.py:222
  986.9 493.8 %reduce-scatter.10.cloned.1.call-start = ((), (), s32[]{:S(2)}) async-start(), calls=%async_computation.11 | async-start | bytes 5898240 | tf_op jit(solution)/shard_map/reduce_scatter | solution.py:240
  994.1 582.9 %reduce-scatter.14.cloned.1.call-start = ((), (), s32[]{:S(2)}) async-start(), calls=%async_computation.13 | async-start | bytes 14155776 | tf_op jit(solution)/shard_map/reduce_scatter | solution.py:242
  1004.8 108.9 %copy-start.162 = (f32[2048]{0:T(1024)S(1)}, f32[2048]{0:T(1024)}, u32[]{:S(2)}) copy-start(f32[2048]{0:T(1024)} %param.36) | copy-start | bytes 24580
  1004.9 108.9 %copy-start.168 = (f32[512]{0:T(512)S(1)}, f32[512]{0:T(512)}, u32[]{:S(2)}) copy-start(f32[512]{0:T(512)} %copy-done.167) | copy-start | bytes 6148
  1007.6 112.8 %copy-start.171 = (f32[2048]{0:T(1024)S(1)}, f32[2048]{0:T(1024)}, u32[]{:S(2)}) copy-start(f32[2048]{0:T(1024)} %get-tuple-element.315) | copy-start | bytes 24580
  1007.6 137.9 %copy-start.176 = (f32[512]{0:T(512)S(1)}, f32[512]{0:T(512)}, u32[]{:S(2)}) copy-start(f32[512]{0:T(512)} %copy-done.175) | copy-start | bytes 6148
  1420.6 158.5 %copy-start.75 = (f32[4,160,160]{2,1,0:T(8,128)S(1)}, f32[4,160,160]{2,1,0:T(8,128)}, u32[]{:S(2)}) copy-start(f32[4,160,160]{2,1,0:T(8,128)} %get-tuple-element.666) | copy-start | bytes 1228804
  (156 other events, 553.2 us)
Sparse Core Ops, SparseCore 0:
  288.1 152.2 all-reduce.128
  442.0 79.7 all-gather.5
  549.2 153.4 all-reduce.130
  704.9 75.7 reduce-scatter.5
  959.4 154.3 all-reduce.132
  1117.1 80.5 reduce-scatter.7
  1201.4 156.8 reduce-scatter.11
  1362.6 57.8 all-reduce.134
  1424.9 55.7 reduce-scatter.9
  1484.6 92.3 reduce-scatter.13
